TPU v7x, 256 devices: a whole 4x4x8 slice. The times are simulated.
256 devices in a mesh: tm: 32 (over y_lo, z, core), gy: 8 (over y_hi, x).
Axes of the slice: x: 4, y: 4 (y_hi: 2, y_lo: 2; y = y_hi * 2 + y_lo), z: 8, core: 2. Of those that a mesh axis runs over, the one named last changes fastest.
Arguments:
- magnetic: bfloat16 [32, 3, 3, 1024, 1024], P('tm', None, None, 'gy'), may hold values from -6 to 6
- velocity: bfloat16 [32, 3, 1, 1024, 1024], P('tm', None, None, 'gy'), may hold values from -6 to 6
- mode_bin: int32 [1024, 1024], P(None, 'gy'), may hold values from 0 to 127, as said below
- omega_edges: int32 [9], replicated, may hold values from 0 to 32, as said below
Outputs:
- power: float32 [32, 1024, 1024], P('tm', None, 'gy')
- spectrum: float32 [8, 128], replicated
Inputs may be any that keep to these rules, and one draw needn't show every extreme that they name: mode_bin = 16 * p + q, where p is a level of min(kz, 1024 - kz) and q a level of min(ky, 1024 - ky); levels never fall as the wavenumber rises, and every value occurs. `omega_edges`: edges rise strictly, the first 0 and the last 32.
All inputs are finite; a program needn't handle non-finite values.
Results may differ from a plain program's by a relative error of at most 0.004.
The roundings to bfloat16 on the way count: a program that leaves them out, or rounds other values in their place, can miss the bound.
Values may be sent and summed in bfloat16 or wider, within the bound.
No kernel may reach another device: no remote copies, remote signals or barrier semaphores. Data moves between devices by JAX's collectives and lax.ppermute only.
A program may use at most 128 MiB of HBM per device.

v0:
```python
import math
import jax
import jax.numpy as jnp
from jax import lax
from jax.sharding import PartitionSpec as P

NBP = 8
NBQ = 16
NB_W = 8
hall_coef = 1.0
highest = lax.Precision.HIGHEST


def extended(cells, sides, width):
    for axis, dim in sides:
        count = lax.axis_size(axis)
        head = lax.slice_in_dim(cells, 0, width, axis=dim)
        tail = lax.slice_in_dim(cells, cells.shape[dim] - width, cells.shape[dim], axis=dim)
        cells = jnp.concatenate(
            [
                lax.ppermute(tail, axis, [(i, (i + 1) % count) for i in range(count)]),
                cells,
                lax.ppermute(head, axis, [((i + 1) % count, i) for i in range(count)]),
            ],
            axis=dim,
        )
    return cells


def window_taper_for(sample_moments, every_time_sample):
    return 0.5 - 0.5 * jnp.cos(
        2.0 * math.pi * (sample_moments.astype(jnp.float32) + 0.5) / every_time_sample
    )


def temporal_coefficients(angular_frequency, sample_moments, every_time_sample):
    phase_angles = jnp.mod(
        angular_frequency[:, None] * sample_moments[None, :], every_time_sample
    ).astype(jnp.float32)
    angles = 2.0 * math.pi * phase_angles / every_time_sample
    taper_weight = window_taper_for(sample_moments, every_time_sample)[None, :]
    return (
        (taper_weight * jnp.cos(angles)).astype(jnp.bfloat16),
        (-taper_weight * jnp.sin(angles)).astype(jnp.bfloat16),
    )


def dft_tables(length):
    series = jnp.arange(length, dtype=jnp.int32)
    phase_angles = jnp.mod(series[:, None] * series[None, :], length).astype(jnp.float32)
    angles = 2.0 * math.pi * phase_angles / length
    return (jnp.cos(angles).astype(jnp.bfloat16), jnp.sin(angles).astype(jnp.bfloat16))


def z_slope(values):
    return (jnp.roll(values, -1, axis=-1) - jnp.roll(values, 1, axis=-1)) * 0.5


def z_turn(re_part, im_part):
    zcos_tab, zsin_tab = dft_tables(re_part.shape[-1])
    turned_re = jnp.dot(re_part, zcos_tab, preferred_element_type=jnp.float32) + jnp.dot(
        im_part, zsin_tab, preferred_element_type=jnp.float32
    )
    turned_im = jnp.dot(im_part, zcos_tab, preferred_element_type=jnp.float32) - jnp.dot(
        re_part, zsin_tab, preferred_element_type=jnp.float32
    )
    return jnp.stack([turned_re, turned_im]).astype(jnp.bfloat16)


def electric_of(magnetic, velocity, slope_magz, slope_magx):
    inner = magnetic[:, :, 1:-1].astype(jnp.float32)
    x_slope = (
        magnetic[:, :, 2:].astype(jnp.float32) - magnetic[:, :, :-2].astype(jnp.float32)
    ) * 0.5
    mag_x, mag_y, mag_z = (inner[:, 0], inner[:, 1], inner[:, 2])
    cur_x = slope_magz - z_slope(mag_y)
    cur_y = z_slope(mag_x) - x_slope[:, 2]
    cur_z = x_slope[:, 1] - slope_magx
    flow = velocity.astype(jnp.float32)
    vel_x, vel_y, vel_z = (flow[:, 0], flow[:, 1], flow[:, 2])
    elec_x = -(vel_y * mag_z - vel_z * mag_y) + hall_coef * (cur_y * mag_z - cur_z * mag_y)
    elec_y = -(vel_z * mag_x - vel_x * mag_z) + hall_coef * (cur_z * mag_x - cur_x * mag_z)
    elec_z = -(vel_x * mag_y - vel_y * mag_x) + hall_coef * (cur_x * mag_y - cur_y * mag_x)
    return jnp.stack([elec_x, elec_y, elec_z], axis=1)


def body(magnetic, velocity, mode_bin, omega_edges):
    face_rows = jnp.stack([magnetic[:, 2, 1:-1], magnetic[:, 0, 1:-1]], axis=1)
    padded = extended(face_rows, (("gy", 3),), 1)
    slopes = (
        padded[:, :, :, 2:].astype(jnp.float32) - padded[:, :, :, :-2].astype(jnp.float32)
    ) * 0.5
    electric = electric_of(magnetic, velocity, slopes[:, 0], slopes[:, 1]).astype(jnp.bfloat16)
    local_t = electric.shape[0]
    z_count = electric.shape[-1]
    every_time_sample = local_t * lax.axis_size("tm")
    half_count = every_time_sample // 2
    owner_rank = lax.axis_index("tm")
    angular_frequency = owner_rank * local_t + jnp.arange(local_t, dtype=jnp.int32) - half_count
    time_segment = lax.all_gather(electric, "tm", axis=0, tiled=True)
    sample_moments = jnp.arange(time_segment.shape[0], dtype=jnp.int32)
    coefficient_real, coefficient_imaginary = temporal_coefficients(
        angular_frequency, sample_moments, every_time_sample
    )
    re_part = jnp.einsum(
        "wt,tcxyz->wcxyz", coefficient_real, time_segment, preferred_element_type=jnp.float32
    )
    im_part = jnp.einsum(
        "wt,tcxyz->wcxyz", coefficient_imaginary, time_segment, preferred_element_type=jnp.float32
    )
    moved = lax.all_to_all(
        z_turn(re_part.astype(jnp.bfloat16), im_part.astype(jnp.bfloat16)),
        "gy",
        split_axis=5,
        concat_axis=4,
        tiled=True,
    )
    y_count = moved.shape[4]
    ycos_tab, ysin_tab = dft_tables(y_count)
    wave_re = jnp.einsum(
        "wcxyk,yq->wcxqk", moved[0], ycos_tab, preferred_element_type=jnp.float32
    ) + jnp.einsum("wcxyk,yq->wcxqk", moved[1], ysin_tab, preferred_element_type=jnp.float32)
    wave_im = jnp.einsum(
        "wcxyk,yq->wcxqk", moved[1], ycos_tab, preferred_element_type=jnp.float32
    ) - jnp.einsum("wcxyk,yq->wcxqk", moved[0], ysin_tab, preferred_element_type=jnp.float32)
    power_map = jnp.sum(wave_re * wave_re + wave_im * wave_im, axis=(1, 2)) / (
        every_time_sample * y_count * z_count
    )
    kz_local = power_map.shape[2]
    block_rows = min(64, y_count)
    bin_total = NBP * NBQ
    bin_range = jnp.arange(bin_total, dtype=jnp.int32)

    def add_block(step_num, summed):
        row_block = lax.dynamic_slice_in_dim(
            power_map, step_num * block_rows, block_rows, 1
        ).reshape(local_t, block_rows * kz_local)
        bin_ids = lax.dynamic_slice_in_dim(mode_bin, step_num * block_rows, block_rows, 0).reshape(
            block_rows * kz_local
        )
        onehot = (bin_ids[:, None] == bin_range[None, :]).astype(jnp.float32)
        return summed + jnp.dot(row_block, onehot, precision=highest)

    by_mode = lax.fori_loop(
        0, y_count // block_rows, add_block, jnp.zeros((local_t, bin_total), jnp.float32)
    )
    omega = owner_rank * local_t + jnp.arange(local_t, dtype=jnp.int32)
    member = (
        (omega[None, :] >= omega_edges[:-1, None]) & (omega[None, :] < omega_edges[1:, None])
    ).astype(jnp.float32)
    partial_value = jnp.dot(member, by_mode, precision=highest)
    binned = lax.psum(partial_value, ("tm", "gy"))
    spectrum = jnp.log(
        binned * (NB_W * bin_total) / (every_time_sample * y_count * z_count) + 1e-06
    )
    return (power_map, spectrum)


def solution(mesh):
    return jax.shard_map(
        body,
        mesh=mesh,
        in_specs=(
            P("tm", None, None, "gy", None),
            P("tm", None, None, "gy", None),
            P(None, "gy"),
            P(),
        ),
        out_specs=(P("tm", None, "gy"), P()),
        check_vma=False,
    )
```

profile of v0, /device:TPU:1, one launch (start us, length us, event | category | flops | bytes accessed | tf_op | source)
XLA Modules:
  0.0 512.5 jit_solution(18000967554781323091)
XLA Ops:
  8.5 6.0 %collective-permute-start = (bf16[1,2,1,1,1024]{4,3,2,1,0:T(2,128)(2,1)S(1)}, bf16[1,2,1,1,1024]{4,3,2,1,0:T(2,128)(2,1)S(1)}, u32[]{:S(2)}, u32[]{:S(2)}) collective-permute-start(bf16[1,2,1,1,1024]{4,3,2,1,0:T(2,128)(2,1)S(1)} %get-tuple-element.139), channel_id=1, source_target_pairs={{1,0},{2,1},{3,2},{4,3},{5,4},{6,5},{7,6},{0,7},{9,8},{10,9},{11,1... | collective-permute-start | bytes 12296 | tf_op jit(solution)/shard_map/ppermute | solution.py:23
  16.7 3.9 collective-permute-done.1
  23.7 142.3 %all-gather.2.cloned.1.call-done = bf16[32,3,1,128,1024]{4,3,2,1,0:T(8,128)(2,1)} async-done(((bf16[1,3,1,128,1024]{4,3,2,1,0:T(8,128)(2,1)}), bf16[32,3,1,128,1024]{4,3,2,1,0:T(8,128)(2,1)}) %all-gather.2.cloned.1.call-update) | async-done | bytes 25165840 | tf_op jit(solution)/shard_map/all_gather | solution.py:100
  166.0 24.4 %fusion.5 = bf16[1,3,128,1024]{3,0,2,1:T(2,128)(2,1)S(1)} fusion(bf16[32,3,128,1024]{3,2,1,0:T(8,128)(2,1)} %bitcast.97, s32[]{:T(128)S(6)} %sub.139), kind=kOutput, calls=%fused_computation.8 | convolution fusion | flops 25166528 | bytes 25952260 | tf_op jit(solution)/shard_map/wt,tcxyz->wcxyz/dot_general | solution.py:108
  190.5 24.9 %fusion.7 = bf16[1,3,128,1024]{3,0,2,1:T(2,128)(2,1)S(1)} fusion(bf16[32,3,128,1024]{3,2,1,0:T(8,128)(2,1)} %bitcast.98, s32[]{:T(128)S(6)} %sub.139), kind=kOutput, calls=%fused_computation.10 | convolution fusion | flops 25166496 | bytes 25952260 | tf_op jit(solution)/shard_map/wt,tcxyz->wcxyz/dot_general | solution.py:105
  215.4 16.1 %fusion.21 = f32[3,128,1024]{2,1,0:T(8,128)S(1)} fusion(bf16[1,3,128,1024]{3,0,2,1:T(2,128)(2,1)S(1)} %fusion.7), kind=kOutput, calls=%fused_computation.27 | convolution fusion | flops 821035008 | bytes 2359296 | tf_op jit(solution)/shard_map/dot_general | solution.py:64
  231.5 16.1 %fusion.23 = f32[3,128,1024]{2,1,0:T(8,128)S(1)} fusion(bf16[1,3,128,1024]{3,0,2,1:T(2,128)(2,1)S(1)} %fusion.5), kind=kOutput, calls=%fused_computation.28 | convolution fusion | flops 821035008 | bytes 2359296 | tf_op jit(solution)/shard_map/dot_general | solution.py:61
  247.6 16.5 %fusion.42 = bf16[1,1,3,1,128,1024]{5,4,2,3,1,0:T(8,128)(2,1)S(1)} fusion(f32[3,128,1024]{2,1,0:T(8,128)S(1)} %fusion.21, bf16[1,3,128,1024]{3,0,2,1:T(2,128)(2,1)S(1)} %fusion.5), kind=kOutput, calls=%fused_computation.41 | convolution fusion | flops 821821440 | bytes 3145728 | tf_op jit(solution)/shard_map/dot_general | solution.py:64
  264.1 16.3 %fusion.39 = bf16[1,1,3,1,128,1024]{5,4,2,3,1,0:T(8,128)(2,1)S(1)} fusion(f32[3,128,1024]{2,1,0:T(8,128)S(1)} %fusion.23, bf16[1,3,128,1024]{3,0,2,1:T(2,128)(2,1)S(1)} %fusion.7), kind=kOutput, calls=%fused_computation.40 | convolution fusion | flops 821821440 | bytes 3145728 | tf_op jit(solution)/shard_map/dot_general | solution.py:61
  280.6 3.0 copy.44
  283.6 6.7 %all-to-all-start = ((bf16[2,1,3,1,128,1024]{4,0,3,2,1,5:T(2,128)(2,1)}), bf16[2,1,3,1,128,1024]{4,0,3,2,1,5:T(2,128)(2,1)S(1)}, u32[]{:S(2)}, u32[]{:S(2)}) async-start(bf16[2,1,3,1,128,1024]{4,0,3,2,1,5:T(2,128)(2,1)} %copy.44), calls=%async_computation | async-start | bytes 3145728 | tf_op jit(solution)/shard_map/all_to_all | solution.py:111
  290.4 22.9 %all-to-all-done = bf16[2,1,3,1,128,1024]{4,0,3,2,1,5:T(2,128)(2,1)S(1)} async-done(((bf16[2,1,3,1,128,1024]{4,0,3,2,1,5:T(2,128)(2,1)}), bf16[2,1,3,1,128,1024]{4,0,3,2,1,5:T(2,128)(2,1)S(1)}, u32[]{:S(2)}, u32[]{:S(2)}) %all-to-all-start) | async-done | bytes 1572896 | tf_op jit(solution)/shard_map/all_to_all | solution.py:111
  313.3 2.4 copy.45
  315.8 17.9 %fusion.29 = f32[1024,3,128]{2,0,1:T(8,128)S(1)} fusion(bf16[3,1024,128]{2,1,0:T(8,128)(2,1)S(1)} %bitcast.104), kind=kOutput, calls=%fused_computation.31 | convolution fusion | flops 821035008 | bytes 2359296 | tf_op jit(solution)/shard_map/wcxyk,yq->wcxqk/dot_general | solution.py:123
  333.7 18.0 %fusion.19 = f32[1024,3,128]{2,0,1:T(8,128)S(1)} fusion(bf16[3,1024,128]{2,1,0:T(8,128)(2,1)S(1)} %bitcast.105), kind=kOutput, calls=%fused_computation.26 | convolution fusion | flops 821035008 | bytes 2359296 | tf_op jit(solution)/shard_map/wcxyk,yq->wcxqk/dot_general | solution.py:122
  351.6 18.0 %fusion.17 = f32[1024,3,128]{2,0,1:T(8,128)S(1)} fusion(bf16[3,1024,128]{2,1,0:T(8,128)(2,1)S(1)} %bitcast.102), kind=kOutput, calls=%fused_computation.25 | convolution fusion | flops 821035008 | bytes 2359296 | tf_op jit(solution)/shard_map/wcxyk,yq->wcxqk/dot_general | solution.py:125
  369.6 18.0 %add_reduce_fusion = f32[1024,128]{1,0:T(8,128)S(1)} fusion(f32[1024,3,128]{2,0,1:T(8,128)S(1)} %fusion.29, f32[1024,3,128]{2,0,1:T(8,128)S(1)} %fusion.17, f32[1024,3,128]{2,0,1:T(8,128)S(1)} %fusion.19, bf16[3,1024,128]{2,1,0:T(8,128)(2,1)S(1)} %bitcast.103), kind=kOutput, calls=%fused_computation.36 | convolution fusion | flops 823263232 | bytes 6029312 | tf_op jit(solution)/shard_map/wcxyk,yq->wcxqk/dot_general | solution.py:120
  387.7 41.5 %while.14 = (s32[]{:T(128)}, f32[1,128]{1,0:T(1,128)S(1)}, f32[1,1024,128]{2,1,0:T(8,128)S(1)}, s32[1024,128]{1,0:T(8,128)}, s32[]{:T(128)}, /*index=5*/s32[]{:T(128)}, s32[]{:T(128)}, s32[]{:T(128)}) while((s32[]{:T(128)}, f32[1,128]{1,0:T(1,128)S(1)}, f32[1,1024,128]{2,1,0:T(8,128)S(1)}, s32[1024,128]{1,0:T(8,128)}, s32[]{:T(128)}, ...), condition=%wide.region_2.3_spmd.clone, body=%wide.region_1.2_spmd.clone.sunk | while | flops 13631751 | bytes 197789 | solution.py:144
  388.5 1.8 fusion.113
  393.7 1.8 fusion.113
  396.3 1.8 fusion.113
  398.9 1.8 fusion.113
  401.5 1.8 fusion.113
  404.1 1.8 fusion.113
  406.6 1.8 fusion.113
  409.2 1.8 fusion.113
  414.4 1.8 fusion.113
  417.0 1.8 fusion.113
  422.2 1.8 fusion.113
  424.8 1.8 fusion.113
  427.4 1.8 fusion.113
  429.3 75.6 %psum.7 = f32[8,128]{1,0:T(8,128)S(1)} all-reduce(f32[8,128]{1,0:T(8,128)S(1)} %broadcast_multiply_fusion), channel_id=1, replica_groups=mesh['tm'=32,'gy'=8] {'tm','gy'}, use_global_device_ids=true, to_apply=%region_3.4 | all-reduce | flops 1024 | bytes 8192 | tf_op jit(solution)/shard_map/psum | solution.py:152
  (69 shorter events, 25.3 us)
Async XLA Ops:
  7.2 8.7 %copy-start = (bf16[1,3,3,128,1024]{4,3,2,1,0:T(8,128)(2,1)S(1)}, bf16[1,3,3,128,1024]{4,3,2,1,0:T(8,128)(2,1)}, u32[]{:S(2)}) copy-start(bf16[1,3,3,128,1024]{4,3,2,1,0:T(8,128)(2,1)} %param.6) | copy-start | bytes 7077892
  7.2 158.9 %all-gather.2.cloned.1.call-start = ((), (), s32[]{:S(2)}) async-start(), calls=%async_computation.1 | async-start | bytes 25952256 | tf_op jit(solution)/shard_map/all_gather | solution.py:100
  8.5 8.2 %collective-permute-start = (bf16[1,2,1,1,1024]{4,3,2,1,0:T(2,128)(2,1)S(1)}, bf16[1,2,1,1,1024]{4,3,2,1,0:T(2,128)(2,1)S(1)}, u32[]{:S(2)}, u32[]{:S(2)}) collective-permute-start(bf16[1,2,1,1,1024]{4,3,2,1,0:T(2,128)(2,1)S(1)} %get-tuple-element.139), channel_id=1, source_target_pairs={{1,0},{2,1},{3,2},{4,3},{5,4},{6,5},{7,6},{0,7},{9,8},{10,9},{11,1... | collective-permute-start | bytes 12296 | tf_op jit(solution)/shard_map/ppermute | solution.py:23
  14.5 2.0 copy-start.2
  14.5 6.1 %collective-permute-start.1 = (bf16[1,2,1,1,1024]{4,3,2,1,0:T(2,128)(2,1)S(1)}, bf16[1,2,1,1,1024]{4,3,2,1,0:T(2,128)(2,1)S(1)}, u32[]{:S(2)}, u32[]{:S(2)}) collective-permute-start(bf16[1,2,1,1,1024]{4,3,2,1,0:T(2,128)(2,1)S(1)} %get-tuple-element.140), channel_id=1, source_target_pairs={{0,1},{1,2},{2,3},{3,4},{4,5},{5,6},{6,7},{7,0},{8,9},{9,10},{10,1... | collective-permute-start | bytes 12296 | tf_op jit(solution)/shard_map/ppermute | solution.py:21
  280.4 9.9 %copy-start.3 = (s32[9]{0:T(128)S(1)}, s32[9]{0:T(128)}, u32[]{:S(2)}) copy-start(s32[9]{0:T(128)} %param.9) | copy-start | bytes 112
  283.6 29.7 %all-to-all-start = ((bf16[2,1,3,1,128,1024]{4,0,3,2,1,5:T(2,128)(2,1)}), bf16[2,1,3,1,128,1024]{4,0,3,2,1,5:T(2,128)(2,1)S(1)}, u32[]{:S(2)}, u32[]{:S(2)}) async-start(bf16[2,1,3,1,128,1024]{4,0,3,2,1,5:T(2,128)(2,1)} %copy.44), calls=%async_computation | async-start | bytes 3145728 | tf_op jit(solution)/shard_map/all_to_all | solution.py:111
  429.2 76.3 %copy-start.1 = (f32[1,1024,128]{2,1,0:T(8,128)}, f32[1,1024,128]{2,1,0:T(8,128)S(1)}, u32[]{:S(2)}) copy-start(f32[1,1024,128]{2,1,0:T(8,128)S(1)} %get-tuple-element.195) | copy-start | bytes 1572868
Sparse Core Ops, SparseCore 0:
  23.8 142.1 all-gather.1
where the time goes:
time: 518 us; the launch traced here: 513 us
  matrix products  215 us (42%)
  waiting for transfers between devices  169 us (33%)
  blocking collectives  75.6 us (15%)
  local copies, waits for them, and re-layouts  19.7 us (4%)
  between operations  14.5 us (3%)
  starting transfers between devices  12.7 us (2%)
  other arithmetic  5.55 us (1%)
    all_gather x1, waiting for transfers between devices, body(): time_segment = lax.all_gather(electric, 'tm', axis=0, tiled=True)  142 us
    psum x1, blocking collectives, body(): binned = lax.psum(partial_value, ('tm', 'gy'))  75.6 us
    dot_general x16, matrix products, add_block(): return summed + jnp.dot(row_block, onehot, precision=highest)  28.7 us
    dot_general x1, matrix products, body(): jnp.einsum('wt,tcxyz->wcxyz', coefficient_real, time_segment, preferred_e...  24.9 us
    dot_general x1, matrix products, body(): jnp.einsum('wt,tcxyz->wcxyz', coefficient_imaginary, time_segment, prefer...  24.4 us
    all_to_all x1, waiting for transfers between devices, body(): lax.all_to_all(z_turn(re_part.astype(jnp.bfloat16), im_part.astype(jnp.bf...  22.9 us
    dot_general x1, matrix products, body(): jnp.einsum('wcxyk,yq->wcxqk', moved[0], ycos_tab, preferred_element_type=...  18 us
    dot_general x1, matrix products, body(): jnp.einsum('wcxyk,yq->wcxqk', moved[1], ysin_tab, preferred_element_type=...  18 us
  transfers between devices with their start and end apart: 4, of which 3 were waited for; matrix products, arithmetic and copies ran while one was open for 0% of the time, Pallas kernels for 0%

commit v1 on v0

--- a/solution.py
+++ b/solution.py
@@ -149,7 +149,7 @@
         (omega[None, :] >= omega_edges[:-1, None]) & (omega[None, :] < omega_edges[1:, None])
     ).astype(jnp.float32)
     partial_value = jnp.dot(member, by_mode, precision=highest)
-    binned = lax.psum(partial_value, ("tm", "gy"))
+    binned = jnp.sum(lax.all_gather(partial_value, ("tm", "gy")), axis=0)
     spectrum = jnp.log(
         binned * (NB_W * bin_total) / (every_time_sample * y_count * z_count) + 1e-06
     )

time: 518 us -> 972 us (1.88)
  waiting for transfers between devices: 169 us -> 697 us
  blocking collectives: 75.6 us -> 0 us
    all_gather x0 -> x1, waiting for transfers between devices: none -> 528 us  [body(): binned = jnp.sum(lax.all_gather(partial_value, ('tm', 'gy')), axis=0)]
    psum x1 -> x0, blocking collectives: 75.6 us -> none  [body(): binned = lax.psum(partial_value, ('tm', 'gy'))]
  transfers between devices with their start and end apart: 4 -> 5, of which waited for: 3 -> 4; matrix products, arithmetic and copies ran while one was open for 0% -> 0% of each run, Pallas kernels for 0% -> 0%
where the time goes in v1:
time: 972 us; the launch traced here: 967 us
  waiting for transfers between devices  697 us (72%)
  matrix products  215 us (22%)
  local copies, waits for them, and re-layouts  19.8 us (2%)
  between operations  14.5 us (1%)
  starting transfers between devices  12.5 us (1%)
    all_gather x1, waiting for transfers between devices, body(): binned = jnp.sum(lax.all_gather(partial_value, ('tm', 'gy')), axis=0)  528 us
    all_gather x1, waiting for transfers between devices, body(): time_segment = lax.all_gather(electric, 'tm', axis=0, tiled=True)  142 us
    dot_general x16, matrix products, add_block(): return summed + jnp.dot(row_block, onehot, precision=highest)  28.7 us
    dot_general x1, matrix products, body(): jnp.einsum('wt,tcxyz->wcxyz', coefficient_real, time_segment, preferred_e...  24.9 us
    dot_general x1, matrix products, body(): jnp.einsum('wt,tcxyz->wcxyz', coefficient_imaginary, time_segment, prefer...  24.4 us
    all_to_all x1, waiting for transfers between devices, body(): lax.all_to_all(z_turn(re_part.astype(jnp.bfloat16), im_part.astype(jnp.bf...  22.9 us
  transfers between devices with their start and end apart: 5, of which 4 were waited for; matrix products, arithmetic and copies ran while one was open for 0% of the time, Pallas kernels for 0%

profile of v1, /device:TPU:1, one launch (start us, length us, event | category | flops | bytes accessed | tf_op | source)
XLA Modules:
  0.0 967.3 jit_solution(4561196361207591041)
XLA Ops:
  8.5 6.0 collective-permute-start
  16.7 3.9 collective-permute-done.1
  23.7 142.3 %all-gather.4.cloned.1.call-done = bf16[32,3,1,128,1024]{4,3,2,1,0:T(8,128)(2,1)} async-done(((bf16[1,3,1,128,1024]{4,3,2,1,0:T(8,128)(2,1)}), bf16[32,3,1,128,1024]{4,3,2,1,0:T(8,128)(2,1)}) %all-gather.4.cloned.1.call-update) | async-done | bytes 25165840 | tf_op jit(solution)/shard_map/all_gather | solution.py:100
  166.1 24.4 %fusion.5 = bf16[1,3,128,1024]{3,0,2,1:T(2,128)(2,1)S(1)} fusion(bf16[32,3,128,1024]{3,2,1,0:T(8,128)(2,1)} %bitcast.99, s32[]{:T(128)S(6)} %sub.139), kind=kOutput, calls=%fused_computation.8 | convolution fusion | flops 25166528 | bytes 25952260 | tf_op jit(solution)/shard_map/wt,tcxyz->wcxyz/dot_general | solution.py:108
  190.5 24.9 %fusion.7 = bf16[1,3,128,1024]{3,0,2,1:T(2,128)(2,1)S(1)} fusion(bf16[32,3,128,1024]{3,2,1,0:T(8,128)(2,1)} %bitcast.100, s32[]{:T(128)S(6)} %sub.139), kind=kOutput, calls=%fused_computation.10 | convolution fusion | flops 25166496 | bytes 25952260 | tf_op jit(solution)/shard_map/wt,tcxyz->wcxyz/dot_general | solution.py:105
  215.4 16.1 %fusion.21 = f32[3,128,1024]{2,1,0:T(8,128)S(1)} fusion(bf16[1,3,128,1024]{3,0,2,1:T(2,128)(2,1)S(1)} %fusion.7), kind=kOutput, calls=%fused_computation.27 | convolution fusion | flops 821035008 | bytes 2359296 | tf_op jit(solution)/shard_map/dot_general | solution.py:64
  231.5 16.1 %fusion.23 = f32[3,128,1024]{2,1,0:T(8,128)S(1)} fusion(bf16[1,3,128,1024]{3,0,2,1:T(2,128)(2,1)S(1)} %fusion.5), kind=kOutput, calls=%fused_computation.28 | convolution fusion | flops 821035008 | bytes 2359296 | tf_op jit(solution)/shard_map/dot_general | solution.py:61
  247.6 16.5 %fusion.42 = bf16[1,1,3,1,128,1024]{5,4,2,3,1,0:T(8,128)(2,1)S(1)} fusion(f32[3,128,1024]{2,1,0:T(8,128)S(1)} %fusion.21, bf16[1,3,128,1024]{3,0,2,1:T(2,128)(2,1)S(1)} %fusion.5), kind=kOutput, calls=%fused_computation.41 | convolution fusion | flops 821821440 | bytes 3145728 | tf_op jit(solution)/shard_map/dot_general | solution.py:64
  264.1 16.3 %fusion.39 = bf16[1,1,3,1,128,1024]{5,4,2,3,1,0:T(8,128)(2,1)S(1)} fusion(f32[3,128,1024]{2,1,0:T(8,128)S(1)} %fusion.23, bf16[1,3,128,1024]{3,0,2,1:T(2,128)(2,1)S(1)} %fusion.7), kind=kOutput, calls=%fused_computation.40 | convolution fusion | flops 821821440 | bytes 3145728 | tf_op jit(solution)/shard_map/dot_general | solution.py:61
  280.6 3.0 copy.54
  283.6 6.4 all-to-all-start
  290.2 22.9 %all-to-all-done = bf16[2,1,3,1,128,1024]{4,0,3,2,1,5:T(2,128)(2,1)S(1)} async-done(((bf16[2,1,3,1,128,1024]{4,0,3,2,1,5:T(2,128)(2,1)}), bf16[2,1,3,1,128,1024]{4,0,3,2,1,5:T(2,128)(2,1)S(1)}, u32[]{:S(2)}, u32[]{:S(2)}) %all-to-all-start) | async-done | bytes 1572896 | tf_op jit(solution)/shard_map/all_to_all | solution.py:111
  313.1 2.6 copy.55
  315.7 17.9 %fusion.29 = f32[1024,3,128]{2,0,1:T(8,128)S(1)} fusion(bf16[3,1024,128]{2,1,0:T(8,128)(2,1)S(1)} %bitcast.106), kind=kOutput, calls=%fused_computation.31 | convolution fusion | flops 821035008 | bytes 2359296 | tf_op jit(solution)/shard_map/wcxyk,yq->wcxqk/dot_general | solution.py:123
  333.6 18.0 %fusion.19 = f32[1024,3,128]{2,0,1:T(8,128)S(1)} fusion(bf16[3,1024,128]{2,1,0:T(8,128)(2,1)S(1)} %bitcast.107), kind=kOutput, calls=%fused_computation.26 | convolution fusion | flops 821035008 | bytes 2359296 | tf_op jit(solution)/shard_map/wcxyk,yq->wcxqk/dot_general | solution.py:122
  351.6 18.0 %fusion.17 = f32[1024,3,128]{2,0,1:T(8,128)S(1)} fusion(bf16[3,1024,128]{2,1,0:T(8,128)(2,1)S(1)} %bitcast.104), kind=kOutput, calls=%fused_computation.25 | convolution fusion | flops 821035008 | bytes 2359296 | tf_op jit(solution)/shard_map/wcxyk,yq->wcxqk/dot_general | solution.py:125
  369.6 18.0 %add_reduce_fusion = f32[1024,128]{1,0:T(8,128)S(1)} fusion(f32[1024,3,128]{2,0,1:T(8,128)S(1)} %fusion.29, f32[1024,3,128]{2,0,1:T(8,128)S(1)} %fusion.17, f32[1024,3,128]{2,0,1:T(8,128)S(1)} %fusion.19, bf16[3,1024,128]{2,1,0:T(8,128)(2,1)S(1)} %bitcast.105), kind=kOutput, calls=%fused_computation.36 | convolution fusion | flops 823263232 | bytes 6029312 | tf_op jit(solution)/shard_map/wcxyk,yq->wcxqk/dot_general | solution.py:120
  387.7 41.5 %while.14 = (s32[]{:T(128)}, f32[1,128]{1,0:T(1,128)S(1)}, f32[1,1024,128]{2,1,0:T(8,128)S(1)}, s32[1024,128]{1,0:T(8,128)}, s32[]{:T(128)}, /*index=5*/s32[]{:T(128)}, s32[]{:T(128)}, s32[]{:T(128)}) while((s32[]{:T(128)}, f32[1,128]{1,0:T(1,128)S(1)}, f32[1,1024,128]{2,1,0:T(8,128)S(1)}, s32[1024,128]{1,0:T(8,128)}, s32[]{:T(128)}, ...), condition=%wide.region_2.3_spmd.clone, body=%wide.region_1.2_spmd.clone.sunk | while | flops 13631751 | bytes 197789 | solution.py:144
  391.1 1.8 fusion.113
  393.7 1.8 fusion.113
  396.2 1.8 fusion.113
  398.8 1.8 fusion.113
  401.4 1.8 fusion.113
  404.0 1.8 fusion.113
  406.6 1.8 fusion.113
  411.8 1.8 fusion.113
  414.4 1.8 fusion.113
  417.0 1.8 fusion.113
  419.6 1.8 fusion.113
  422.2 1.8 fusion.113
  424.7 1.8 fusion.113
  429.9 528.2 %all-gather.6.cloned.1.call-done = f32[2048,128]{1,0:T(8,128)} async-done(((f32[8,128]{1,0:T(8,128)}), f32[2048,128]{1,0:T(8,128)}) %all-gather.6.cloned.1.call-update) | async-done | bytes 1048592 | tf_op jit(solution)/shard_map/all_gather | solution.py:152
  (72 shorter events, 27.5 us)
Async XLA Ops:
  7.2 8.7 copy-start
  7.2 158.9 %all-gather.4.cloned.1.call-start = ((), (), s32[]{:S(2)}) async-start(), calls=%async_computation.1 | async-start | bytes 25952256 | tf_op jit(solution)/shard_map/all_gather | solution.py:100
  8.5 8.2 collective-permute-start
  14.5 2.0 copy-start.2
  14.5 6.1 collective-permute-start.1
  280.4 9.7 %copy-start.3 = (s32[9]{0:T(128)S(1)}, s32[9]{0:T(128)}, u32[]{:S(2)}) copy-start(s32[9]{0:T(128)} %param.9) | copy-start | bytes 112
  283.6 29.4 %all-to-all-start = ((bf16[2,1,3,1,128,1024]{4,0,3,2,1,5:T(2,128)(2,1)}), bf16[2,1,3,1,128,1024]{4,0,3,2,1,5:T(2,128)(2,1)S(1)}, u32[]{:S(2)}, u32[]{:S(2)}) async-start(bf16[2,1,3,1,128,1024]{4,0,3,2,1,5:T(2,128)(2,1)} %copy.54), calls=%async_computation | async-start | bytes 3145728 | tf_op jit(solution)/shard_map/all_to_all | solution.py:111
  290.1 668.0 %all-gather.6.cloned.1.call-start = ((), (), s32[]{:S(2)}) async-start(), calls=%async_computation.2 | async-start | bytes 1052672 | tf_op jit(solution)/shard_map/all_gather | solution.py:152
  429.1 531.1 %copy-start.1 = (f32[1,1024,128]{2,1,0:T(8,128)}, f32[1,1024,128]{2,1,0:T(8,128)S(1)}, u32[]{:S(2)}) copy-start(f32[1,1024,128]{2,1,0:T(8,128)S(1)} %get-tuple-element.197) | copy-start | bytes 1572868
Sparse Core Ops, SparseCore 0:
  23.8 142.1 all-gather.3
  430.1 527.9 all-gather.5
